TPU v7x, 32 devices: a whole 2x2x4 slice. The times are simulated.
32 devices in a mesh: row: 8 (over z, x), col: 2 (over core), rank: 2 (over y).
Axes of the slice: x: 2, y: 2, z: 4, core: 2. Of those that a mesh axis runs over, the one named last changes fastest.
Arguments:
- tensor: bfloat16 [64, 2048, 2048], P(None, 'row', 'col'), may hold values from -6 to 6
- aux_factor: bfloat16 [64, 256], P(None, 'rank'), may hold values from -0.75 to 0.75
- row_factor: bfloat16 [2048, 256], P(('row', 'col'), 'rank'), may hold values from -0.125 to 0.125
- col_factor: bfloat16 [2048, 256], P(('col', 'row'), 'rank'), may hold values from -0.125 to 0.125
Outputs:
- row_result: float32 [2048, 256], P(('row', 'col'), 'rank')
- aux_result: float32 [64, 256], P('row', 'rank')
All inputs are finite; a program needn't handle non-finite values.
Results may differ from a plain program's by a relative error of at most 0.0003.
Values may be sent and summed in bfloat16 or wider, within the bound.
A program may use at most 128 MiB of HBM per device.

v0:
```python
import jax
import jax.numpy as jnp
from jax import lax
from jax.sharding import PartitionSpec as P


def reduce_inner(inner, aux_factor, row_panel):
    aux_panel = aux_factor.astype(jnp.float32)
    aux_count = inner.shape[0]
    row_total = jnp.zeros((inner.shape[1], inner.shape[2]), jnp.float32)
    pieces = []
    for start in range(0, aux_count, 8):
        block = inner[start : start + 8]
        row_total = row_total + jnp.sum(block * aux_panel[start : start + 8][:, None, :], axis=0)
        pieces.append(jnp.sum(block * row_panel[None, :, :], axis=1))
    return (row_total, jnp.concatenate(pieces, axis=0))


def body(tensor, aux_factor, row_factor, col_factor):
    row_panel = lax.all_gather(row_factor, "col", axis=0, tiled=True).astype(jnp.float32)
    width = aux_factor.shape[1]
    aux_count = tensor.shape[0]
    orbits = tensor.shape[1]
    flat = tensor.reshape(aux_count * orbits, tensor.shape[2])
    columns = lax.all_gather(col_factor, "row", axis=0, tiled=True)
    inner = jnp.dot(flat, columns, preferred_element_type=jnp.float32)
    inner = inner.reshape(aux_count, orbits, width)
    row_total, aux_total = reduce_inner(inner, aux_factor, row_panel)
    row_result = lax.psum_scatter(row_total, "col", scatter_dimension=0, tiled=True)
    scattered = lax.psum_scatter(aux_total, "row", scatter_dimension=0, tiled=True)
    aux_result = lax.psum(scattered, "col")
    return (row_result, aux_result)


def solution(mesh):
    return jax.shard_map(
        body,
        mesh=mesh,
        in_specs=(
            P(None, "row", "col"),
            P(None, "rank"),
            P(("row", "col"), "rank"),
            P(("col", "row"), "rank"),
        ),
        out_specs=(P(("row", "col"), "rank"), P("row", "rank")),
        check_vma=False,
    )
```

profile of v0, /device:TPU:0, one launch (start us, length us, event | category | flops | bytes accessed | tf_op | source)
XLA Modules:
  0.0 115.6 jit_solution(7216242594102125668)
XLA Ops:
  7.2 0.0 reduce-scatter.2.cloned.1.call-start
  7.2 0.8 fusion.1
  8.0 32.8 %all_gather.6 = bf16[1024,128]{1,0:T(8,128)(2,1)S(1)} all-gather(bf16[128,128]{1,0:T(8,128)(2,1)} %param.7), channel_id=1, replica_groups=mesh['row'=8,'col'=2,'rank'=2] {'row'}, dimensions={0}, use_global_device_ids=true | all-gather | bytes 294912 | tf_op jit(solution)/shard_map/all_gather | solution.py:25
  40.8 0.0 copy-start.1
  40.8 0.0 copy-start.2
  40.8 14.9 %fusion.2 = f32[16384,128]{1,0:T(8,128)S(1)} fusion(bf16[16384,1024]{1,0:T(8,128)(2,1)} %bitcast.20, bf16[1024,128]{1,0:T(8,128)(2,1)S(1)} %all_gather.6), kind=kOutput, calls=%fused_computation.28 | convolution fusion | flops 4294967296 | bytes 42205184 | tf_op jit(solution)/shard_map/dot_general | solution.py:26
  55.7 0.0 copy-start
  55.7 3.2 %copy-done = f32[16384,128]{1,0:T(8,128)} copy-done((f32[16384,128]{1,0:T(8,128)}, f32[16384,128]{1,0:T(8,128)S(1)}, u32[]{:S(2)}) %copy-start) | copy-done | bytes 8388632
  58.9 0.6 fusion
  59.5 0.2 multiply_reduce_fusion.14
  59.6 0.2 multiply_reduce_fusion.8
  59.8 0.2 multiply_reduce_fusion.10
  59.9 0.2 multiply_reduce_fusion.12
  60.1 0.7 add_add_fusion
  60.8 0.0 reduce-scatter.2.cloned.1.call-update
  60.8 0.0 copy-done.1
  60.8 1.9 %all_gather.7 = bf16[256,128]{1,0:T(8,128)(2,1)S(1)} all-gather(bf16[128,128]{1,0:T(8,128)(2,1)S(1)} %copy-done.1), channel_id=1, replica_groups=mesh['row'=8,'col'=2,'rank'=2] {'col'}, dimensions={0}, use_global_device_ids=true | all-gather | bytes 98304 | tf_op jit(solution)/shard_map/all_gather | solution.py:20
  62.7 4.6 %multiply_reduce_fusion = (f32[8,128]{1,0:T(8,128)S(1)}, f32[8,128]{1,0:T(8,128)S(1)}, f32[8,128]{1,0:T(8,128)S(1)}, f32[8,128]{1,0:T(8,128)S(1)}, f32[8,128]{1,...) fusion(f32[256,128]{1,0:T(8,128)S(1)} %convert_element_type.7, f32[16384,128]{1,0:T(8,128)} %copy-done), kind=kLoop, calls=%fused_computation | loop fusion | flops 4186112 | bytes 8552448 | tf_op jit(solution)/shard_map/reduce_sum | solution.py:15
  67.4 0.0 copy-done.2
  67.4 0.6 dynamic-slice
  68.6 37.1 %all-reduce = f32[64,128]{1,0:T(8,128)S(1)} all-reduce(f32[64,128]{1,0:T(8,128)S(1)} %constant_dynamic-update-slice_fusion), channel_id=3, replica_groups=mesh['row'=8,'col'=2,'rank'=2] {'row'}, use_global_device_ids=true, to_apply=%region_17.0.clone | all-reduce | flops 8192 | bytes 65536
  105.7 3.0 %psum.7 = f32[8,128]{1,0:T(8,128)} all-reduce(f32[8,128]{1,0:T(8,128)S(1)} %constant_dynamic-slice_fusion), channel_id=1, replica_groups=mesh['row'=8,'col'=2,'rank'=2] {'col'}, use_global_device_ids=true, to_apply=%region_18.0 | all-reduce | flops 1024 | bytes 8192 | tf_op jit(solution)/shard_map/psum | solution.py:31
  108.8 0.0 reduce-scatter.2.cloned.1.call-done
  (10 shorter events, 0.0 us)
Async XLA Ops:
  7.2 101.6 %reduce-scatter.2.cloned.1.call-start = ((), (), s32[]{:S(2)}) async-start(), calls=%async_computation.1 | async-start | bytes 196608 | tf_op jit(solution)/shard_map/reduce_scatter | solution.py:29
  40.8 20.1 %copy-start.1 = (bf16[128,128]{1,0:T(8,128)(2,1)S(1)}, bf16[128,128]{1,0:T(8,128)(2,1)}, u32[]{:S(2)}) copy-start(bf16[128,128]{1,0:T(8,128)(2,1)} %param.6) | copy-start | bytes 98308
  40.8 26.6 %copy-start.2 = (u32[32]{0:T(128)S(1)}, u32[32]{0:T(128)}, u32[]{:S(2)}) copy-start(u32[32]{0:T(128)} %constant.4) | copy-start | bytes 388
  55.7 3.2 %copy-start = (f32[16384,128]{1,0:T(8,128)}, f32[16384,128]{1,0:T(8,128)S(1)}, u32[]{:S(2)}) copy-start(f32[16384,128]{1,0:T(8,128)S(1)} %fusion.2) | copy-start | bytes 25165828
Sparse Core Ops, SparseCore 0:
  61.0 8.5 reduce-scatter.1
where the time goes:
time: 116 us
  blocking collectives  74.7 us (64%)
  matrix products  14.9 us (13%)
  between operations  14.8 us (13%)
  other arithmetic  5.94 us (5%)
  local copies, waits for them, and re-layouts  5.2 us (4%)
    unnamed x1, blocking collectives  37.1 us
    all_gather x1, blocking collectives, body(): columns = lax.all_gather(col_factor, 'row', axis=0, tiled=True)  32.8 us
    dot_general x1, matrix products, body(): inner = jnp.dot(flat, columns, preferred_element_type=jnp.float32)  14.9 us
    reduce_sum x1, other arithmetic, reduce_inner(): pieces.append(jnp.sum(block * row_panel[None, :, :], axis=1))  4.59 us
    unnamed x15, local copies, waits for them, and re-layouts  3.83 us
    psum x1, blocking collectives, body(): aux_result = lax.psum(scattered, 'col')  3.04 us
  transfers between devices with their start and end apart: 1, of which 0 were waited for; matrix products, arithmetic and copies ran while one was open for 5% of the time, Pallas kernels for 0%

commit v1 on v0

v1 whole, which is shorter than its diff:
```python
import functools

import jax
import jax.numpy as jnp
from jax import lax
from jax.experimental import pallas as pl
from jax.experimental.pallas import tpu as pltpu
from jax.sharding import PartitionSpec as P

MESH = pl.DeviceIdType.MESH
f32 = jnp.float32


def kernel(R, C, tensor, aux, rowf, colf, row_out, aux_out,
           tbuf, colbuf, rowbuf, auxbuf, row_panel, aux_panel, row_acc, aux_acc, row_in, aux_in,
           t_sem, c_send, c_recv, r_send, r_recv, l_sem, a_send, a_recv, p_send, p_recv):
    r = lax.axis_index("row")
    c = lax.axis_index("col")
    other = 1 - c
    A, I, J = tensor.shape
    N = colf.shape[1]
    jb = colf.shape[0]
    ib = rowf.shape[0]
    ac = A // R
    H = R // 2
    jh = J // 2
    half = r // H

    def chunk_of(s):
        return lax.rem(r + 1 + s, R)

    def load(p, s):
        k = chunk_of(s)
        h = half if p == 0 else 1 - half
        cols = pl.ds(pl.multiple_of(h * jh, jh), jh)
        return pltpu.make_async_copy(
            tensor.at[pl.ds(k * ac, ac), :, cols], tbuf.at[p, k], t_sem.at[p, s])

    own_col = pltpu.make_async_copy(colf, colbuf.at[r], l_sem.at[0])
    own_row = pltpu.make_async_copy(rowf, rowbuf.at[c], l_sem.at[1])
    own_aux = pltpu.make_async_copy(aux, auxbuf, l_sem.at[2])
    own_col.start()
    own_row.start()
    own_aux.start()

    barrier = pltpu.get_barrier_semaphore()
    for d in range(R):
        for e in range(C):
            if d or e:
                pl.semaphore_signal(
                    barrier, inc=1, device_id={"row": lax.rem(r + d, R), "col": lax.rem(c + e, C)},
                    device_id_type=MESH)
    for p in range(2):
        for s in range(R):
            load(p, s).start()
    pl.semaphore_wait(barrier, R * C - 1)

    def col_copy(target):
        return pltpu.make_async_remote_copy(
            src_ref=colf, dst_ref=colbuf.at[r], send_sem=c_send.at[target], recv_sem=c_recv.at[r],
            device_id={"row": target}, device_id_type=MESH)

    def col_arrival(source):
        return pltpu.make_async_remote_copy(
            src_ref=colf, dst_ref=colbuf.at[source], send_sem=c_send.at[source], recv_sem=c_recv.at[source],
            device_id={"row": source}, device_id_type=MESH)

    near = [half * H + lax.rem(lax.rem(r, H) + d, H) for d in range(1, H)]
    far = [(1 - half) * H + lax.rem(lax.rem(r, H) + d, H) for d in range(H)]
    for target in near:
        col_copy(target).start()
    row_copy = pltpu.make_async_remote_copy(
        src_ref=rowf, dst_ref=rowbuf.at[c], send_sem=r_send, recv_sem=r_recv,
        device_id={"col": other}, device_id_type=MESH)
    row_copy.start()
    for target in far:
        col_copy(target).start()

    row_acc[...] = jnp.zeros_like(row_acc)
    own_aux.wait()
    aux_panel[...] = auxbuf[...].astype(f32).reshape(R, ac, N)
    own_row.wait()
    row_copy.wait()
    row_panel[...] = rowbuf[...].reshape(C * ib, N).astype(f32)
    own_col.wait()
    for source in near:
        col_arrival(source).wait_recv()

    def block(p, s):
        load(p, s).wait()
        k = chunk_of(s)
        h = half if p == 0 else 1 - half
        weights = colbuf[pl.ds(h * H, H)].reshape(H * jb, N)
        inner = jnp.dot(tbuf[p, k].reshape(ac * I, jh), weights, preferred_element_type=f32).reshape(ac, I, N)
        row_acc[...] += jnp.sum(inner * aux_panel[k][:, None, :], axis=0)
        part = jnp.sum(inner * row_panel[...][None], axis=1)
        if p == 0:
            aux_acc[k] = part
        else:
            aux_acc[k] += part
        return k

    def aux_copy(k, e):
        return pltpu.make_async_remote_copy(
            src_ref=aux_acc.at[k], dst_ref=aux_in.at[r, c], send_sem=a_send.at[k, e], recv_sem=a_recv.at[r, c],
            device_id={"row": k, "col": e}, device_id_type=MESH)

    def aux_arrival(source, e):
        return pltpu.make_async_remote_copy(
            src_ref=aux_acc.at[source], dst_ref=aux_in.at[source, e], send_sem=a_send.at[source, e],
            recv_sem=a_recv.at[source, e], device_id={"row": source, "col": e}, device_id_type=MESH)

    def first(s, _):
        block(0, s)
        return 0

    lax.fori_loop(0, R, first, 0)
    for source in far:
        col_arrival(source).wait_recv()

    def second(s, _):
        k = block(1, s)
        aux_copy(k, c).start()
        aux_copy(k, other).start()
        return 0

    lax.fori_loop(0, R - 1, second, 0)
    block(1, R - 1)
    part_copy = pltpu.make_async_remote_copy(
        src_ref=row_acc.at[pl.ds(other * ib, ib)], dst_ref=row_in, send_sem=p_send, recv_sem=p_recv,
        device_id={"col": other}, device_id_type=MESH)
    part_copy.start()
    aux_copy(r, other).start()
    aux_in[r, c] = aux_acc[r]
    for d in range(1, R):
        source = lax.rem(r + d, R)
        for e in range(C):
            aux_arrival(source, e).wait_recv()
    aux_arrival(r, other).wait_recv()
    aux_out[...] = jnp.sum(aux_in[...].reshape(R * C, ac, N), axis=0)
    part_copy.wait_recv()
    row_out[...] = row_acc[pl.ds(c * ib, ib)] + row_in[...]

    part_copy.wait_send()
    aux_copy(r, other).wait_send()
    for d in range(1, R):
        k = lax.rem(r + d, R)
        col_copy(k).wait_send()
        for e in range(C):
            aux_copy(k, e).wait_send()


def fused(R, C, tensor, aux, rowf, colf):
    A, I, J = tensor.shape
    jb, N = colf.shape
    ib = rowf.shape[0]
    ac = A // R
    bf16 = tensor.dtype
    anywhere = pl.BlockSpec(memory_space=pltpu.HBM)
    vmem = pl.BlockSpec(memory_space=pltpu.VMEM)
    dma = pltpu.SemaphoreType.DMA
    return pl.pallas_call(
        functools.partial(kernel, R, C),
        out_shape=(jax.ShapeDtypeStruct((ib, N), f32), jax.ShapeDtypeStruct((ac, N), f32)),
        in_specs=[anywhere] * 4,
        out_specs=(vmem, vmem),
        scratch_shapes=[
            pltpu.VMEM((2, R, ac, I, J // 2), bf16),
            pltpu.VMEM((R, jb, N), bf16),
            pltpu.VMEM((C, ib, N), bf16),
            pltpu.VMEM((A, N), bf16),
            pltpu.VMEM((C * ib, N), f32),
            pltpu.VMEM((R, ac, N), f32),
            pltpu.VMEM((C * ib, N), f32),
            pltpu.VMEM((R, ac, N), f32),
            pltpu.VMEM((ib, N), f32),
            pltpu.VMEM((R, C, ac, N), f32),
            dma((2, R)), dma((R,)), dma((R,)), dma, dma, dma((3,)),
            dma((R, C)), dma((R, C)), dma, dma,
        ],
        compiler_params=pltpu.CompilerParams(
            collective_id=0, has_side_effects=True, vmem_limit_bytes=58 * 2**20),
    )(tensor, aux, rowf, colf)


def plain(tensor, aux_factor, row_factor, col_factor):
    row_panel = lax.all_gather(row_factor, "col", axis=0, tiled=True).astype(f32)
    columns = lax.all_gather(col_factor, "row", axis=0, tiled=True)
    A, I, J = tensor.shape
    inner = jnp.dot(tensor.reshape(A * I, J), columns, preferred_element_type=f32).reshape(A, I, -1)
    row_total = jnp.sum(inner * aux_factor.astype(f32)[:, None, :], axis=0)
    aux_total = jnp.sum(inner * row_panel[None], axis=1)
    row_result = lax.psum_scatter(row_total, "col", scatter_dimension=0, tiled=True)
    scattered = lax.psum_scatter(aux_total, "row", scatter_dimension=0, tiled=True)
    return row_result, lax.psum(scattered, "col")


def solution(mesh):
    R, C = mesh.shape["row"], mesh.shape["col"]

    def body(tensor, aux, rowf, colf):
        A, I, J = tensor.shape
        jb, N = colf.shape
        ib = rowf.shape[0]
        fits = (C == 2 and R % 2 == 0 and A % (8 * R) == 0 and ib % 16 == 0 and jb % 16 == 0
                and J % 256 == 0 and N % 128 == 0 and 2 * tensor.size < 48 * 2**20)
        if fits:
            return tuple(fused(R, C, tensor, aux, rowf, colf))
        return plain(tensor, aux, rowf, colf)

    return jax.shard_map(
        body,
        mesh=mesh,
        in_specs=(
            P(None, "row", "col"),
            P(None, "rank"),
            P(("row", "col"), "rank"),
            P(("col", "row"), "rank"),
        ),
        out_specs=(P(("row", "col"), "rank"), P("row", "rank")),
        check_vma=False,
    )
```

time: 116 us -> 29.4 us (0.25)
  blocking collectives: 74.7 us -> 0 us
  Pallas kernels: 0 us -> 25.8 us
  matrix products: 14.9 us -> 0 us
  between operations: 14.8 us -> 0.64 us
  other arithmetic: 5.94 us -> 0 us
  local copies, waits for them, and re-layouts: 5.2 us -> 2.74 us
    unnamed x1 -> x0, blocking collectives: 37.1 us -> none
    all_gather x2 -> x0, blocking collectives: 34.6 us -> none  [the longest x1 32.8 us: body(): columns = lax.all_gather(col_factor, 'row', axis=0, tiled=True)]
    pallas_call x0 -> x1, Pallas kernels: none -> 25.8 us  [fused(): pl.pallas_call(functools.partial(kernel, R, C), out_shape=(jax.ShapeDtype...]
    dot_general x1 -> x0, matrix products: 14.9 us -> none  [body(): inner = jnp.dot(flat, columns, preferred_element_type=jnp.float32)]
    reduce_sum x5 -> x0, other arithmetic: 5.23 us -> none  [the longest x1 4.59 us: reduce_inner(): pieces.append(jnp.sum(block * row_panel[None, :, :], axis=1))]
    psum x1 -> x0, blocking collectives: 3.04 us -> none  [body(): aux_result = lax.psum(scattered, 'col')]
    slice x2 -> x0, local copies, waits for them, and re-layouts: 1.37 us -> none  [the longest x1 0.8 us: reduce_inner(): aux_panel[start:start + 8][:, None, :]]
    unnamed x15 -> x2, local copies, waits for them, and re-layouts: 3.83 us -> 2.74 us
  transfers between devices with their start and end apart: 1 -> 0, of which waited for: 0 -> 0; matrix products, arithmetic and copies ran while one was open for 5% -> 0% of each run, Pallas kernels for 0% -> 0%
where the time goes in v1:
time: 29.4 us; the launch traced here: 29.2 us
  Pallas kernels  25.8 us (88%)
  local copies, waits for them, and re-layouts  2.74 us (9%)
  between operations  0.64 us (2%)
    pallas_call x1, Pallas kernels, fused(): pl.pallas_call(functools.partial(kernel, R, C), out_shape=(jax.ShapeDtype...  25.8 us
    unnamed x2, local copies, waits for them, and re-layouts  2.74 us

profile of v1, /device:TPU:0, one launch (start us, length us, event | category | flops | bytes accessed | tf_op | source)
XLA Modules:
  0.0 29.2 jit_solution(124866288459756209)
XLA Ops:
  0.6 25.8 %shard_map.59 = (f32[128,128]{1,0:T(8,128)}, f32[8,128]{1,0:T(8,128)}) custom-call(bf16[64,256,1024]{2,1,0:T(8,128)(2,1)} %tensor.1, bf16[64,128]{1,0:T(8,128)(2,1)} %aux.1, bf16[128,128]{1,0:T(8,128)(2,1)} %rowf.1, bf16[128,128]{1,0:T(8,128)(2,1)} %colf.1), custom_call_target="tpu_custom_call" | custom-call | tf_op jit(solution)/shard_map/pallas_call | solution.py:162
  26.5 1.5 %copy.8 = f32[128,128]{1,0:T(8,128)} copy(f32[128,128]{1,0:T(8,128)} %get-tuple-element.4) | data formatting | bytes 131072
  27.9 1.3 %copy.9 = f32[8,128]{1,0:T(8,128)} copy(f32[8,128]{1,0:T(8,128)} %get-tuple-element.5) | data formatting | bytes 8192

commit v2 on v1

--- a/solution.py
+++ b/solution.py
@@ -11,9 +11,9 @@
 f32 = jnp.float32
 
 
-def kernel(R, C, tensor, aux, rowf, colf, row_out, aux_out,
-           tbuf, colbuf, rowbuf, auxbuf, row_panel, aux_panel, row_acc, aux_acc, row_in, aux_in,
-           t_sem, c_send, c_recv, r_send, r_recv, l_sem, a_send, a_recv, p_send, p_recv):
+def kernel(R, C, tensor, aux, rowf, colf, out,
+           tbuf, colbuf, rowbuf, auxbuf, row_panel, aux_panel, row_acc, aux_acc, inner_acc, row_in, aux_in,
+           t_sem, c_send, c_recv, r_send, r_recv, l_sem, a_send, a_recv, p_send, p_recv, far_sem):
     r = lax.axis_index("row")
     c = lax.axis_index("col")
     other = 1 - c
@@ -44,16 +44,28 @@
     own_aux.start()
 
     barrier = pltpu.get_barrier_semaphore()
-    for d in range(R):
-        for e in range(C):
-            if d or e:
-                pl.semaphore_signal(
-                    barrier, inc=1, device_id={"row": lax.rem(r + d, R), "col": lax.rem(c + e, C)},
-                    device_id_type=MESH)
+    near = [half * H + lax.rem(lax.rem(r, H) + d, H) for d in range(1, H)]
+    far = [(1 - half) * H + lax.rem(lax.rem(r, H) + d, H) for d in range(H)]
+    x = lax.rem(r, 2)
+    gate = jnp.where(half == 0, H - 2, H) + x
+    beyond = jnp.where(half == 0, H, H - 2) + x
+    at_gate = r == gate
+
+    def signal(sem, where):
+        pl.semaphore_signal(sem, inc=1, device_id=where, device_id_type=MESH)
+
+    signal(barrier, {"col": other})
+    for target in near:
+        signal(barrier, {"row": target})
+
+    @pl.when(at_gate)
+    def _():
+        signal(barrier, {"row": beyond})
+
     for p in range(2):
         for s in range(R):
             load(p, s).start()
-    pl.semaphore_wait(barrier, R * C - 1)
+    pl.semaphore_wait(barrier, H + jnp.where(at_gate, 1, 0))
 
     def col_copy(target):
         return pltpu.make_async_remote_copy(
@@ -65,14 +77,24 @@
             src_ref=colf, dst_ref=colbuf.at[source], send_sem=c_send.at[source], recv_sem=c_recv.at[source],
             device_id={"row": source}, device_id_type=MESH)
 
-    near = [half * H + lax.rem(lax.rem(r, H) + d, H) for d in range(1, H)]
-    far = [(1 - half) * H + lax.rem(lax.rem(r, H) + d, H) for d in range(H)]
     for target in near:
         col_copy(target).start()
     row_copy = pltpu.make_async_remote_copy(
         src_ref=rowf, dst_ref=rowbuf.at[c], send_sem=r_send, recv_sem=r_recv,
         device_id={"col": other}, device_id_type=MESH)
     row_copy.start()
+
+    @pl.when(at_gate)
+    def _():
+        signal(far_sem, {"row": beyond})
+
+    pl.semaphore_wait(far_sem, 1)
+
+    @pl.when(at_gate)
+    def _():
+        for d in range(1, H // 2):
+            signal(far_sem, {"row": half * H + lax.rem(lax.rem(r, H) + 2 * d, H)})
+
     for target in far:
         col_copy(target).start()
 
@@ -86,18 +108,18 @@
     for source in near:
         col_arrival(source).wait_recv()
 
-    def block(p, s):
+    def product(p, s):
         load(p, s).wait()
         k = chunk_of(s)
         h = half if p == 0 else 1 - half
         weights = colbuf[pl.ds(h * H, H)].reshape(H * jb, N)
-        inner = jnp.dot(tbuf[p, k].reshape(ac * I, jh), weights, preferred_element_type=f32).reshape(ac, I, N)
+        return k, jnp.dot(tbuf[p, k].reshape(ac * I, jh), weights, preferred_element_type=f32)
+
+    def block(s):
+        k, inner = product(1, s)
+        inner = (inner_acc[k] + inner).reshape(ac, I, N)
         row_acc[...] += jnp.sum(inner * aux_panel[k][:, None, :], axis=0)
-        part = jnp.sum(inner * row_panel[...][None], axis=1)
-        if p == 0:
-            aux_acc[k] = part
-        else:
-            aux_acc[k] += part
+        aux_acc[k] = jnp.sum(inner * row_panel[...][None], axis=1)
         return k
 
     def aux_copy(k, e):
@@ -111,7 +133,8 @@
             recv_sem=a_recv.at[source, e], device_id={"row": source, "col": e}, device_id_type=MESH)
 
     def first(s, _):
-        block(0, s)
+        k, inner = product(0, s)
+        inner_acc[k] = inner
         return 0
 
     lax.fori_loop(0, R, first, 0)
@@ -119,13 +142,13 @@
         col_arrival(source).wait_recv()
 
     def second(s, _):
-        k = block(1, s)
+        k = block(s)
         aux_copy(k, c).start()
         aux_copy(k, other).start()
         return 0
 
     lax.fori_loop(0, R - 1, second, 0)
-    block(1, R - 1)
+    block(R - 1)
     part_copy = pltpu.make_async_remote_copy(
         src_ref=row_acc.at[pl.ds(other * ib, ib)], dst_ref=row_in, send_sem=p_send, recv_sem=p_recv,
         device_id={"col": other}, device_id_type=MESH)
@@ -137,9 +160,9 @@
         for e in range(C):
             aux_arrival(source, e).wait_recv()
     aux_arrival(r, other).wait_recv()
-    aux_out[...] = jnp.sum(aux_in[...].reshape(R * C, ac, N), axis=0)
+    out[ib:, :] = jnp.sum(aux_in[...].reshape(R * C, ac, N), axis=0)
     part_copy.wait_recv()
-    row_out[...] = row_acc[pl.ds(c * ib, ib)] + row_in[...]
+    out[:ib, :] = row_acc[pl.ds(c * ib, ib)] + row_in[...]
 
     part_copy.wait_send()
     aux_copy(r, other).wait_send()
@@ -148,6 +171,12 @@
         col_copy(k).wait_send()
         for e in range(C):
             aux_copy(k, e).wait_send()
+
+
+def split(both, row_out, aux_out):
+    rows = row_out.shape[0]
+    row_out[...] = both[:rows, :]
+    aux_out[...] = both[rows:, :]
 
 
 def fused(R, C, tensor, aux, rowf, colf):
@@ -159,11 +188,11 @@
     anywhere = pl.BlockSpec(memory_space=pltpu.HBM)
     vmem = pl.BlockSpec(memory_space=pltpu.VMEM)
     dma = pltpu.SemaphoreType.DMA
-    return pl.pallas_call(
+    both = pl.pallas_call(
         functools.partial(kernel, R, C),
-        out_shape=(jax.ShapeDtypeStruct((ib, N), f32), jax.ShapeDtypeStruct((ac, N), f32)),
+        out_shape=jax.ShapeDtypeStruct((ib + ac, N), f32),
         in_specs=[anywhere] * 4,
-        out_specs=(vmem, vmem),
+        out_specs=vmem,
         scratch_shapes=[
             pltpu.VMEM((2, R, ac, I, J // 2), bf16),
             pltpu.VMEM((R, jb, N), bf16),
@@ -173,14 +202,21 @@
             pltpu.VMEM((R, ac, N), f32),
             pltpu.VMEM((C * ib, N), f32),
             pltpu.VMEM((R, ac, N), f32),
+            pltpu.VMEM((R, ac * I, N), f32),
             pltpu.VMEM((ib, N), f32),
             pltpu.VMEM((R, C, ac, N), f32),
             dma((2, R)), dma((R,)), dma((R,)), dma, dma, dma((3,)),
-            dma((R, C)), dma((R, C)), dma, dma,
+            dma((R, C)), dma((R, C)), dma, dma, pltpu.SemaphoreType.REGULAR,
         ],
         compiler_params=pltpu.CompilerParams(
-            collective_id=0, has_side_effects=True, vmem_limit_bytes=58 * 2**20),
+            collective_id=0, has_side_effects=True, vmem_limit_bytes=56 * 2**20),
     )(tensor, aux, rowf, colf)
+    return pl.pallas_call(
+        split,
+        out_shape=(jax.ShapeDtypeStruct((ib, N), f32), jax.ShapeDtypeStruct((ac, N), f32)),
+        in_specs=[vmem],
+        out_specs=(vmem, vmem),
+    )(both)
 
 
 def plain(tensor, aux_factor, row_factor, col_factor):
@@ -202,8 +238,8 @@
         A, I, J = tensor.shape
         jb, N = colf.shape
         ib = rowf.shape[0]
-        fits = (C == 2 and R % 2 == 0 and A % (8 * R) == 0 and ib % 16 == 0 and jb % 16 == 0
-                and J % 256 == 0 and N % 128 == 0 and 2 * tensor.size < 48 * 2**20)
+        fits = (C == 2 and R % 4 == 0 and A % (8 * R) == 0 and ib % 16 == 0 and jb % 16 == 0
+                and J % 256 == 0 and N % 128 == 0 and 2 * tensor.size < 36 * 2**20)
         if fits:
             return tuple(fused(R, C, tensor, aux, rowf, colf))
         return plain(tensor, aux, rowf, colf)

time: 29.4 us -> 25.1 us (0.85)
  local copies, waits for them, and re-layouts: 2.74 us -> 0 us
  Pallas kernels: 25.8 us -> 24.3 us
    unnamed x2 -> x0, local copies, waits for them, and re-layouts: 2.74 us -> none
    pallas_call x1 -> x2, Pallas kernels: 25.8 us -> 24.3 us  [the longest x1 22.7 us: fused(): pl.pallas_call(functools.partial(kernel, R, C), out_shape=jax.ShapeDtypeS...]
where the time goes in v2:
time: 25.1 us; the launch traced here: 24.9 us
  Pallas kernels  24.3 us (97%)
  between operations  0.64 us (3%)
    pallas_call x1, Pallas kernels, fused(): pl.pallas_call(functools.partial(kernel, R, C), out_shape=jax.ShapeDtypeS...  22.7 us
    pallas_call x1, Pallas kernels, fused(): pl.pallas_call(split, out_shape=(jax.ShapeDtypeStruct((ib, N), f32), jax....  1.52 us

profile of v2, /device:TPU:0, one launch (start us, length us, event | category | flops | bytes accessed | tf_op | source)
XLA Modules:
  0.0 24.9 jit_solution(6836899757730165084)
XLA Ops:
  0.6 22.7 %shard_map.59.both = f32[136,128]{1,0:T(8,128)} custom-call(bf16[64,256,1024]{2,1,0:T(8,128)(2,1)} %tensor.1, bf16[64,128]{1,0:T(8,128)(2,1)} %aux.1, bf16[128,128]{1,0:T(8,128)(2,1)} %rowf.1, bf16[128,128]{1,0:T(8,128)(2,1)} %colf.1), custom_call_target="tpu_custom_call" | custom-call | tf_op jit(solution)/shard_map/pallas_call | solution.py:191
  23.4 1.5 %shard_map.60 = (f32[128,128]{1,0:T(8,128)}, f32[8,128]{1,0:T(8,128)}) custom-call(f32[136,128]{1,0:T(8,128)} %shard_map.59.both), custom_call_target="tpu_custom_call" | custom-call | tf_op jit(solution)/shard_map/pallas_call | solution.py:214
